TPU v7x, 256 devices: a whole 4x4x8 slice. The times are simulated.
256 devices in a mesh: pipe: 8 (over z), dp: 2 (over y_lo), expert: 16 (over y_hi, x, core).
Axes of the slice: x: 4, y: 4 (y_hi: 2, y_lo: 2; y = y_hi * 2 + y_lo), z: 8, core: 2. Of those that a mesh axis runs over, the one named last changes fastest.
Arguments:
- layer_input: bfloat16 [8, 4096, 1536], P('pipe', ('dp', 'expert')), may hold values from -6 to 6
- handoff: bfloat16 [8, 4096, 1536], P('pipe', ('dp', 'expert')), may hold values from -6 to 6
- routes: int32 [8, 4096, 2], P('pipe', ('dp', 'expert')), may hold values from 0 to 7, all different within a row; in each aligned block of 128 rows (0 to 127, 128 to 255, ..., all dimensions but the last counted through in order) at most 48 rows name the same one
- gating: bfloat16 [8, 4096, 2], P('pipe', ('dp', 'expert')), may hold values from 0.19921875 to 1
- saved_pre: bfloat16 [8, 2, 16, 32, 48, 768], P('pipe', 'dp', 'expert'), may hold values from -6 to 6
- w_in: bfloat16 [8, 1536, 2, 16, 768], P('pipe', None, 'dp', 'expert'), may hold values from -0.15625 to 0.15625
- w_out: bfloat16 [8, 2, 16, 768, 1536], P('pipe', 'dp', 'expert'), may hold values from -0.109375 to 0.109375
Outputs:
- token_grad: bfloat16 [8, 4096, 1536], P('pipe', ('dp', 'expert'))
- w_in_grad: bfloat16 [8, 1536, 2, 16, 768], P('pipe', None, 'dp', 'expert')
- w_out_grad: bfloat16 [8, 2, 16, 768, 1536], P('pipe', 'dp', 'expert')
Inputs may be any that keep to these rules, and one draw needn't show every extreme that they name: `routes`: each token names two different experts. In each block of 128 tokens (the tokens of one device) no expert is named more than 48 times, and in every block some expert is named exactly 48 times.
All inputs are finite; a program needn't handle non-finite values.
Results may differ from a plain program's by a relative error of at most 0.0049.
Values may be sent and summed in bfloat16 or wider, within the bound.
No kernel may reach another device: no remote copies, remote signals or barrier semaphores. Data moves between devices by JAX's collectives and lax.ppermute only.
A program may use at most 128 MiB of HBM per device.

v0:
```python
import math

import jax
import jax.numpy as jnp
from jax import lax
from jax.sharding import PartitionSpec as P

root_two_pi = math.sqrt(2.0 / math.pi)
cubic_coef = 0.044715


def from_behind(value, axis, steps):
    count = lax.axis_size(axis)
    pairs = [(source, (source + steps) % count) for source in range(count)]
    return lax.ppermute(value, axis, pairs)


def gelu_parts(values):
    inner_arg = root_two_pi * (values + cubic_coef * values * values * values)
    tangent = jnp.tanh(inner_arg)
    active = 0.5 * values * (1.0 + tangent)
    gelu_slope = 0.5 * (1.0 + tangent) + 0.5 * values * (1.0 - tangent * tangent) * root_two_pi * (
        1.0 + 3.0 * cubic_coef * values * values
    )
    return (active, gelu_slope)


def slot_table(route_block, expert_total, capacity):
    flat_ids = route_block.reshape(-1)
    pair_total = flat_ids.shape[0]
    onehot = (flat_ids[:, None] == jnp.arange(expert_total, dtype=jnp.int32)[None, :]).astype(
        jnp.int32
    )
    running = jnp.cumsum(onehot, axis=0) - 1
    position = jnp.sum(running * onehot, axis=1)
    slot_index = jnp.full((expert_total, capacity), pair_total, jnp.int32)
    slot_index = slot_index.at[flat_ids, position].set(jnp.arange(pair_total, dtype=jnp.int32))
    return (flat_ids, position, slot_index)


def fill_slots(source_rows, slot_index):
    padded = jnp.concatenate(
        [source_rows, jnp.zeros((1, source_rows.shape[1]), source_rows.dtype)], axis=0
    )
    return padded[slot_index // 2]


def expert_backward(input_rows, grad_rows, gate_rows, pre_panels, win_panels, wout_panels):
    upstream = jnp.einsum("rd,phd->prh", grad_rows, wout_panels, preferred_element_type=jnp.float32)
    active, gelu_slope = gelu_parts(pre_panels.astype(jnp.float32))
    weight = gate_rows.astype(jnp.float32)[None, :, None]
    scaled = (weight * active).astype(jnp.bfloat16)
    pre_grad = (weight * upstream * gelu_slope).astype(jnp.bfloat16)
    out_grad = jnp.einsum("prh,rd->phd", scaled, grad_rows, preferred_element_type=jnp.float32)
    in_grad = jnp.einsum("rd,prh->pdh", input_rows, pre_grad, preferred_element_type=jnp.float32)
    row_grad = jnp.einsum("prh,dph->rd", pre_grad, win_panels, preferred_element_type=jnp.float32)
    return (in_grad, out_grad, row_grad)


def on_device(layer_input, handoff, routes, gating, saved_pre, w_in, w_out):
    expert_count = lax.axis_size("expert")
    expert_total = expert_count // 2
    capacity = saved_pre.shape[4]
    panel_size = w_in.shape[4]
    model_width = w_in.shape[1]
    incoming = from_behind(handoff, "pipe", -1)
    grad_tokens = incoming[0]
    input_tokens = layer_input[0]
    flat_ids, position, slot_index = slot_table(routes[0], expert_total, capacity)
    input_slots = fill_slots(input_tokens, slot_index)
    grad_slots = fill_slots(grad_tokens, slot_index)
    gate_padded = jnp.concatenate([gating[0].reshape(-1), jnp.zeros((1,), gating.dtype)], axis=0)
    gate_slots = gate_padded[slot_index]
    recv_input, recv_grad, recv_gate = (
        lax.all_to_all(
            jnp.repeat(input_slots, 2, axis=0), "expert", split_axis=0, concat_axis=0, tiled=True
        ),
        lax.all_to_all(
            jnp.repeat(grad_slots, 2, axis=0), "expert", split_axis=0, concat_axis=0, tiled=True
        ),
        lax.all_to_all(
            jnp.repeat(gate_slots, 2, axis=0), "expert", split_axis=0, concat_axis=0, tiled=True
        ),
    )
    win_all, wout_all, pre_all = (
        lax.all_gather(w_in, "dp", axis=2, tiled=True),
        lax.all_gather(w_out, "dp", axis=1, tiled=True),
        lax.all_gather(saved_pre, "dp", axis=1, tiled=True),
    )
    dp_count = lax.axis_size("dp")
    own_index = lax.axis_index("dp")
    pre_own = lax.dynamic_slice_in_dim(pre_all, own_index * expert_count, expert_count, 3)
    row_total = expert_count * capacity
    in_grad, out_grad, row_grad = expert_backward(
        recv_input.reshape(row_total, model_width),
        recv_grad.reshape(row_total, model_width),
        recv_gate.reshape(row_total),
        pre_own.reshape(dp_count, row_total, panel_size),
        win_all.reshape(model_width, dp_count, panel_size),
        wout_all.reshape(dp_count, panel_size, model_width),
    )
    in_share, out_share = (
        lax.psum_scatter(in_grad, "dp", scatter_dimension=0, tiled=True),
        lax.psum_scatter(out_grad, "dp", scatter_dimension=0, tiled=True),
    )
    partial_rows = row_grad.reshape(expert_count, capacity, model_width)
    w_in_grad = in_share.astype(jnp.bfloat16).reshape(w_in.shape)
    w_out_grad = out_share.astype(jnp.bfloat16).reshape(w_out.shape)
    returned = lax.all_to_all(partial_rows, "expert", split_axis=0, concat_axis=0, tiled=True)
    expert_rows = returned.reshape(expert_total, 2, capacity, model_width).sum(axis=1)
    flat_rows = expert_rows.reshape(expert_total * capacity, model_width)
    picked = flat_rows[flat_ids * capacity + position]
    token_total = grad_tokens.shape[0]
    moe_grad = picked.reshape(token_total, 2, model_width).sum(axis=1)
    token_grad = (grad_tokens.astype(jnp.float32) + moe_grad).astype(jnp.bfloat16)[None]
    return (token_grad, w_in_grad, w_out_grad)


def solution(mesh):
    in_specs = (
        P("pipe", ("dp", "expert"), None),
        P("pipe", ("dp", "expert"), None),
        P("pipe", ("dp", "expert"), None),
        P("pipe", ("dp", "expert"), None),
        P("pipe", "dp", "expert", None, None, None),
        P("pipe", None, "dp", "expert", None),
        P("pipe", "dp", "expert", None, None),
    )
    out_specs = (
        P("pipe", ("dp", "expert"), None),
        P("pipe", None, "dp", "expert", None),
        P("pipe", "dp", "expert", None, None),
    )
    return jax.shard_map(
        on_device, mesh=mesh, in_specs=in_specs, out_specs=out_specs, check_vma=False
    )
```

profile of v0, /device:TPU:1, one launch (start us, length us, event | category | flops | bytes accessed | tf_op | source)
XLA Modules:
  0.0 572.4 jit_solution(1482647437347051874)
XLA Ops:
  8.7 6.5 %collective-permute-start = (bf16[1,128,1536]{2,1,0:T(8,128)(2,1)S(1)}, bf16[1,128,1536]{2,1,0:T(8,128)(2,1)S(1)}, u32[]{:S(2)}, u32[]{:S(2)}) collective-permute-start(bf16[1,128,1536]{2,1,0:T(8,128)(2,1)S(1)} %copy-done.3), channel_id=1, source_target_pairs={{0,224},{32,0},{64,32},{96,64},{128,96},{160,128},{192,160},{224,1... | collective-permute-start | bytes 1179656 | tf_op jit(solution)/shard_map/ppermute | solution.py:15
  16.7 11.2 %scatter_fusion = s32[8,48]{1,0:T(8,128)S(1)} fusion(s32[8,48]{1,0:T(8,128)S(1)} %broadcast_in_dim.12, s32[256]{0:T(256)S(1)} %bitcast.80, s32[256]{0:T(256)S(1)} %iota.11), kind=kCustom, calls=%fused_computation.4 | custom fusion | bytes 5120 | tf_op jit(solution)/shard_map/scatter | solution.py:37
  28.3 2.8 gather_fusion
  31.8 7.9 %all-to-all-start = ((bf16[16,1,48]{2,1,0:T(2,128)(2,1)}), bf16[16,1,48]{2,1,0:T(2,128)(2,1)S(1)}, u32[]{:S(2)}, u32[]{:S(2)}) async-start(bf16[16,1,48]{2,1,0:T(2,128)(2,1)} %copy.40), calls=%async_computation | async-start | bytes 16384 | tf_op jit(solution)/shard_map/all_to_all | solution.py:81
  42.1 4.6 all-to-all-done
  48.3 4.8 all-to-all-start.1
  56.2 33.2 %all-to-all-done.1 = bf16[16,48,1536]{2,1,0:T(8,128)(2,1)} async-done(((bf16[16,48,1536]{2,1,0:T(8,128)(2,1)}), bf16[16,48,1536]{2,1,0:T(8,128)(2,1)}, u32[]{:S(2)}, u32[]{:S(2)}) %all-to-all-start.1) | async-done | bytes 2359328 | tf_op jit(solution)/shard_map/all_to_all | solution.py:78
  91.0 4.5 all-to-all-start.3
  95.9 35.9 %all-gather.6.cloned.1.call-done = bf16[1,2,1,32,48,768]{5,4,3,2,0,1:T(8,128)(2,1)} async-done(((bf16[1,1,1,32,48,768]{5,4,3,2,0,1:T(8,128)(2,1)}), bf16[1,2,1,32,48,768]{5,4,3,2,0,1:T(8,128)(2,1)}) %all-gather.6.cloned.1.call-update) | async-done | bytes 4718608 | tf_op jit(solution)/shard_map/all_gather | solution.py:88
  131.8 3.2 constant_dynamic-slice_fusion
  135.1 67.4 %all-gather.4.cloned.1.call-done = bf16[1,2,1,768,1536]{4,3,2,0,1:T(8,128)(2,1)} async-done(((bf16[1,1,1,768,1536]{4,3,2,0,1:T(8,128)(2,1)}), bf16[1,2,1,768,1536]{4,3,2,0,1:T(8,128)(2,1)}) %all-gather.4.cloned.1.call-update) | async-done | bytes 4718608 | tf_op jit(solution)/shard_map/all_gather | solution.py:87
  202.4 11.3 %fusion.6 = bf16[2,768,768]{2,1,0:T(8,128)(2,1)} fusion(bf16[1,2,1,16,48,768]{5,4,3,2,0,1:T(8,128)(2,1)} %constant_dynamic-slice_fusion, f32[768]{0:T(1024)S(1)} %reshape.162, bf16[768,1536,1]{1,0,2:T(8,128)(2,1)} %bitcast.9, bf16[1,2,1,768,1536]{4,3,2,0,1:T(8,128)(2,1)} %all-gather.4.cloned.1.call-done), kind=kOutput, calls=%fused_computation.15 | convolution fusion | flops 3648651264 | bytes 11799552 | tf_op jit(solution)/shard_map/rd,phd->prh/dot_general | solution.py:49
  213.8 8.1 %convolution_bitcast_fusion = f32[2,1536,768]{1,2,0:T(8,128)} fusion(bf16[2,768,768]{2,1,0:T(8,128)(2,1)} %fusion.6, bf16[768,1536,1]{1,0,2:T(8,128)(2,1)S(1)} %bitcast.87), kind=kOutput, calls=%fused_computation.8 | convolution fusion | flops 3623878656 | bytes 14155776 | tf_op jit(solution)/shard_map/rd,prh->pdh/dot_general | solution.py:55
  221.9 3.2 fusion.12
  225.1 8.1 %fusion.30 = f32[2,768,1536]{2,1,0:T(8,128)} fusion(bf16[2,768,768]{2,1,0:T(8,128)(2,1)S(1)} %bitcast.83, bf16[768,1536,1]{1,0,2:T(8,128)(2,1)} %bitcast.9), kind=kOutput, calls=%fused_computation.64 | convolution fusion | flops 3623878656 | bytes 14155776 | tf_op jit(solution)/shard_map/prh,rd->phd/dot_general | solution.py:54
  233.3 39.7 %all-gather.8.cloned.1.call-done = bf16[1,1536,2,1,768]{4,1,3,0,2:T(8,128)(2,1)} async-done(((bf16[1,1536,1,1,768]{4,1,3,0,2:T(8,128)(2,1)}), bf16[1,1536,2,1,768]{4,1,3,0,2:T(8,128)(2,1)}) %all-gather.8.cloned.1.call-update) | async-done | bytes 4718608 | tf_op jit(solution)/shard_map/all_gather | solution.py:86
  273.0 7.8 %fusion.19 = f32[16,48,1536]{2,1,0:T(8,128)} fusion(bf16[16,48,768,2]{2,1,0,3:T(8,128)(2,1)S(1)} %bitcast.94, bf16[1,1536,2,1,768]{4,1,3,0,2:T(8,128)(2,1)} %all-gather.8.cloned.1.call-done), kind=kOutput, calls=%fused_computation.31 | convolution fusion | flops 3623878656 | bytes 11796480 | tf_op jit(solution)/shard_map/prh,dph->rd/dot_general | solution.py:56
  280.8 7.3 %all-to-all-start.2 = ((f32[16,48,1536]{2,1,0:T(8,128)}), f32[16,48,1536]{2,1,0:T(8,128)}, u32[]{:S(2)}, u32[]{:S(2)}) async-start(f32[16,48,1536]{2,1,0:T(8,128)} %fusion.19), calls=%async_computation.2 | async-start | bytes 9437184 | tf_op jit(solution)/shard_map/all_to_all | solution.py:109
  288.1 67.6 %all-to-all-done.2 = f32[16,48,1536]{2,1,0:T(8,128)} async-done(((f32[16,48,1536]{2,1,0:T(8,128)}), f32[16,48,1536]{2,1,0:T(8,128)}, u32[]{:S(2)}, u32[]{:S(2)}) %all-to-all-start.2) | async-done | bytes 4718624 | tf_op jit(solution)/shard_map/all_to_all | solution.py:109
  355.7 3.0 bitcast_reduce_fusion
  366.0 76.6 %reduce-scatter.3.cloned.1.call-done = f32[1,1536,768]{1,2,0:T(8,128)} async-done(((f32[2,1536,768]{1,2,0:T(8,128)}), f32[1,1536,768]{1,2,0:T(8,128)}) %reduce-scatter.3.cloned.1.call-update) | async-done | bytes 4718608 | tf_op jit(solution)/shard_map/reduce_scatter | solution.py:103
  442.6 2.6 convert_bitcast_fusion.1
  447.6 114.2 %reduce-scatter.5.cloned.1.call-done = f32[1,768,1536]{2,1,0:T(8,128)} async-done(((f32[2,768,1536]{2,1,0:T(8,128)}), f32[1,768,1536]{2,1,0:T(8,128)}) %reduce-scatter.5.cloned.1.call-update) | async-done | bytes 4718608 | tf_op jit(solution)/shard_map/reduce_scatter | solution.py:104
  561.8 4.0 convert_bitcast_fusion
  (61 shorter events, 22.8 us)
Async XLA Ops:
  7.2 1.5 copy-start.3
  7.2 8.0 %copy-start.1 = (s32[1,128,2]{1,2,0:T(2,128)S(1)}, s32[1,128,2]{1,2,0:T(2,128)}, u32[]{:S(2)}) copy-start(s32[1,128,2]{1,2,0:T(2,128)} %param.9) | copy-start | bytes 3076
  7.2 20.7 %copy-start.2 = (bf16[1,128,2]{1,2,0:T(2,128)(2,1)S(1)}, bf16[1,128,2]{1,2,0:T(2,128)(2,1)}, u32[]{:S(2)}) copy-start(bf16[1,128,2]{1,2,0:T(2,128)(2,1)} %param.10) | copy-start | bytes 1540
  7.2 124.6 %all-gather.6.cloned.1.call-start = ((), (), s32[]{:S(2)}) async-start(), calls=%async_computation.7 | async-start | bytes 7077888 | tf_op jit(solution)/shard_map/all_gather | solution.py:88
  7.9 194.5 %all-gather.4.cloned.1.call-start = ((), (), s32[]{:S(2)}) async-start(), calls=%async_computation.6 | async-start | bytes 7077888 | tf_op jit(solution)/shard_map/all_gather | solution.py:87
  8.7 31.1 %collective-permute-start = (bf16[1,128,1536]{2,1,0:T(8,128)(2,1)S(1)}, bf16[1,128,1536]{2,1,0:T(8,128)(2,1)S(1)}, u32[]{:S(2)}, u32[]{:S(2)}) collective-permute-start(bf16[1,128,1536]{2,1,0:T(8,128)(2,1)S(1)} %copy-done.3), channel_id=1, source_target_pairs={{0,224},{32,0},{64,32},{96,64},{128,96},{160,128},{192,160},{224,1... | collective-permute-start | bytes 1179656 | tf_op jit(solution)/shard_map/ppermute | solution.py:15
  31.8 14.8 %all-to-all-start = ((bf16[16,1,48]{2,1,0:T(2,128)(2,1)}), bf16[16,1,48]{2,1,0:T(2,128)(2,1)S(1)}, u32[]{:S(2)}, u32[]{:S(2)}) async-start(bf16[16,1,48]{2,1,0:T(2,128)(2,1)} %copy.40), calls=%async_computation | async-start | bytes 16384 | tf_op jit(solution)/shard_map/all_to_all | solution.py:81
  46.7 7.2 %copy-start = (bf16[1,128,1536]{2,1,0:T(8,128)(2,1)S(1)}, bf16[1,128,1536]{2,1,0:T(8,128)(2,1)}, u32[]{:S(2)}) copy-start(bf16[1,128,1536]{2,1,0:T(8,128)(2,1)} %param.7) | copy-start | bytes 1179652
  48.3 41.0 %all-to-all-start.1 = ((bf16[16,48,1536]{2,1,0:T(8,128)(2,1)}), bf16[16,48,1536]{2,1,0:T(8,128)(2,1)}, u32[]{:S(2)}, u32[]{:S(2)}) async-start(bf16[16,48,1536]{2,1,0:T(8,128)(2,1)} %bitcast.7), calls=%async_computation.1 | async-start | bytes 4718592 | tf_op jit(solution)/shard_map/all_to_all | solution.py:78
  53.2 219.8 %all-gather.8.cloned.1.call-start = ((), (), s32[]{:S(2)}) async-start(), calls=%async_computation.8 | async-start | bytes 7077888 | tf_op jit(solution)/shard_map/all_gather | solution.py:86
  91.0 122.7 %all-to-all-start.3 = ((bf16[16,48,1536]{2,1,0:T(8,128)(2,1)}), bf16[16,48,1536]{2,1,0:T(8,128)(2,1)S(1)}, u32[]{:S(2)}, u32[]{:S(2)}) async-start(bf16[16,48,1536]{2,1,0:T(8,128)(2,1)} %bitcast.28), calls=%async_computation.3 | async-start | bytes 4718592 | tf_op jit(solution)/shard_map/all_to_all | solution.py:75
  95.6 347.0 %reduce-scatter.3.cloned.1.call-start = ((), (), s32[]{:S(2)}) async-start(), calls=%async_computation.9 | async-start | bytes 14155776 | tf_op jit(solution)/shard_map/reduce_scatter | solution.py:103
  221.9 340.0 %reduce-scatter.5.cloned.1.call-start = ((), (), s32[]{:S(2)}) async-start(), calls=%async_computation.10 | async-start | bytes 14155776 | tf_op jit(solution)/shard_map/reduce_scatter | solution.py:104
  233.2 39.7 %copy-start.4 = (bf16[2,768,768]{2,1,0:T(8,128)(2,1)S(1)}, bf16[2,768,768]{2,1,0:T(8,128)(2,1)}, u32[]{:S(2)}) copy-start(bf16[2,768,768]{2,1,0:T(8,128)(2,1)} %fusion.6) | copy-start | bytes 7077892
  280.8 74.9 %all-to-all-start.2 = ((f32[16,48,1536]{2,1,0:T(8,128)}), f32[16,48,1536]{2,1,0:T(8,128)}, u32[]{:S(2)}, u32[]{:S(2)}) async-start(f32[16,48,1536]{2,1,0:T(8,128)} %fusion.19), calls=%async_computation.2 | async-start | bytes 9437184 | tf_op jit(solution)/shard_map/all_to_all | solution.py:109
Sparse Core Ops, SparseCore 0:
  9.8 121.9 all-gather.5
  133.6 68.7 all-gather.3
  204.2 68.7 all-gather.7
  275.4 167.1 reduce-scatter.2
  445.0 116.8 reduce-scatter.4
where the time goes:
time: 573 us; the launch traced here: 572 us
  waiting for transfers between devices  441 us (77%)
  matrix products  35.3 us (6%)
  local copies, waits for them, and re-layouts  34.1 us (6%)
  starting transfers between devices  31.4 us (5%)
  other arithmetic  16.3 us (3%)
  between operations  14 us (2%)
    reduce_scatter x1, waiting for transfers between devices, on_device(): lax.psum_scatter(out_grad, 'dp', scatter_dimension=0, tiled=True)  114 us
    reduce_scatter x1, waiting for transfers between devices, on_device(): lax.psum_scatter(in_grad, 'dp', scatter_dimension=0, tiled=True)  76.6 us
    all_to_all x1, waiting for transfers between devices, on_device(): lax.all_to_all(partial_rows, 'expert', split_axis=0, concat_axis=0, tiled...  67.6 us
    all_gather x1, waiting for transfers between devices, on_device(): lax.all_gather(w_out, 'dp', axis=1, tiled=True)  67.4 us
    all_gather x1, waiting for transfers between devices, on_device(): lax.all_gather(w_in, 'dp', axis=2, tiled=True)  39.7 us
    all_gather x1, waiting for transfers between devices, on_device(): lax.all_gather(saved_pre, 'dp', axis=1, tiled=True)  35.9 us
    all_to_all x1, waiting for transfers between devices, on_device(): lax.all_to_all(jnp.repeat(grad_slots, 2, axis=0), 'expert', split_axis=0,...  33.2 us
  transfers between devices with their start and end apart: 10, of which 8 were waited for; matrix products, arithmetic and copies ran while one was open for 14% of the time, Pallas kernels for 0%

commit v1 on v0

v1 whole, which is shorter than its diff:
```python
import math

import jax
import jax.numpy as jnp
from jax import lax
from jax.sharding import PartitionSpec as P

root_two_pi = math.sqrt(2.0 / math.pi)
cubic_coef = 0.044715


def gelu_parts(values):
    square = values * values
    tangent = jnp.tanh(root_two_pi * values * (1.0 + cubic_coef * square))
    half = 0.5 * (1.0 + tangent)
    slope = half + 0.5 * values * (1.0 - tangent * tangent) * root_two_pi * (
        1.0 + 3.0 * cubic_coef * square
    )
    return (values * half, slope)


def slot_keys(route_block, capacity):
    flat_ids = route_block.reshape(-1)
    pair_total = flat_ids.shape[0]
    order = jnp.arange(pair_total, dtype=jnp.int32)
    earlier = (flat_ids[:, None] == flat_ids[None, :]) & (order[:, None] < order[None, :])
    position = jnp.sum(earlier.astype(jnp.int32), axis=0)
    return (flat_ids * capacity + position).reshape(route_block.shape)


def on_device(layer_input, handoff, routes, gating, saved_pre, w_in, w_out):
    pipe_count = lax.axis_size("pipe")
    expert_count = lax.axis_size("expert")
    dp_count = lax.axis_size("dp")
    expert_total = expert_count // 2
    blocks, capacity, panel_size = saved_pre.shape[3:]
    model_width = w_in.shape[1]
    half = capacity // 2
    slots = expert_total * capacity
    everyone = ("dp", "expert")

    incoming = lax.ppermute(
        handoff, "pipe", [(s, (s - 1) % pipe_count) for s in range(pipe_count)]
    )
    grad_tokens = incoming[0]
    input_tokens = layer_input[0]
    keys = slot_keys(routes[0], capacity)
    slot_ids = jnp.arange(slots, dtype=jnp.int32)[:, None]
    first = slot_ids == keys[:, 0][None, :]
    second = slot_ids == keys[:, 1][None, :]
    chosen = (first | second).astype(jnp.bfloat16)
    gates = gating[0]
    zero = jnp.zeros((), jnp.bfloat16)
    gated = jnp.where(first, gates[:, 0][None, :], zero) + jnp.where(
        second, gates[:, 1][None, :], zero
    )

    def dispatch(select, tokens):
        rows = jnp.dot(select, tokens, preferred_element_type=jnp.float32).astype(jnp.bfloat16)
        rows = rows.reshape(1, expert_count, half, model_width)
        sent = jnp.broadcast_to(rows, (dp_count, expert_count, half, model_width))
        sent = sent.reshape(dp_count * expert_count, half, model_width)
        return lax.all_to_all(sent, everyone, split_axis=0, concat_axis=0, tiled=True)

    swap = [(e, e ^ 1) for e in range(expert_count)]

    def both(own):
        other = lax.ppermute(own, "expert", swap)
        return jnp.concatenate(
            [own.reshape(-1, own.shape[-1]), other.reshape(-1, own.shape[-1])], axis=0
        )

    grad_rows = both(dispatch(gated, grad_tokens))
    input_rows = both(dispatch(chosen, input_tokens))

    core = lax.axis_index("expert") % 2
    pre = saved_pre.reshape(blocks, 2, half, panel_size)
    pre_own = lax.dynamic_index_in_dim(pre, core, 1, keepdims=False)
    pre_other = lax.dynamic_index_in_dim(pre, 1 - core, 1, keepdims=False)
    pre_rows = jnp.concatenate([pre_own, pre_other], axis=0).reshape(-1, panel_size)
    win = w_in.reshape(model_width, panel_size)
    wout = w_out.reshape(panel_size, model_width)

    upstream = jnp.einsum("rd,hd->rh", grad_rows, wout, preferred_element_type=jnp.float32)
    active, slope = gelu_parts(pre_rows.astype(jnp.float32))
    pre_grad = (upstream * slope).astype(jnp.bfloat16)
    row_grad = jnp.einsum("rh,dh->rd", pre_grad, win, preferred_element_type=jnp.float32)
    row_total = blocks * half
    mine = row_grad[:row_total]
    theirs = row_grad[row_total:].astype(jnp.bfloat16)
    summed = mine + lax.ppermute(theirs, "expert", swap).astype(jnp.float32)
    back = lax.all_to_all(
        summed.astype(jnp.bfloat16).reshape(blocks, half, model_width),
        everyone,
        split_axis=0,
        concat_axis=0,
        tiled=True,
    )
    out_grad = jnp.einsum(
        "rh,rd->hd", active.astype(jnp.bfloat16), grad_rows, preferred_element_type=jnp.float32
    )
    in_grad = jnp.einsum("rd,rh->dh", input_rows, pre_grad, preferred_element_type=jnp.float32)

    back = back.reshape(dp_count, slots, model_width)
    moe_grad = jnp.einsum(
        "st,psd->td", chosen, back, preferred_element_type=jnp.float32
    )
    token_grad = (grad_tokens.astype(jnp.float32) + moe_grad).astype(jnp.bfloat16)[None]
    return (
        token_grad,
        in_grad.astype(jnp.bfloat16).reshape(w_in.shape),
        out_grad.astype(jnp.bfloat16).reshape(w_out.shape),
    )


def solution(mesh):
    in_specs = (
        P("pipe", ("dp", "expert"), None),
        P("pipe", ("dp", "expert"), None),
        P("pipe", ("dp", "expert"), None),
        P("pipe", ("dp", "expert"), None),
        P("pipe", "dp", "expert", None, None, None),
        P("pipe", None, "dp", "expert", None),
        P("pipe", "dp", "expert", None, None),
    )
    out_specs = (
        P("pipe", ("dp", "expert"), None),
        P("pipe", None, "dp", "expert", None),
        P("pipe", "dp", "expert", None, None),
    )
    return jax.shard_map(
        on_device, mesh=mesh, in_specs=in_specs, out_specs=out_specs, check_vma=False
    )
```

time: 573 us -> 142 us (0.25)
  waiting for transfers between devices: 441 us -> 31.1 us
  blocking collectives: 0 us -> 40.2 us
  local copies, waits for them, and re-layouts: 34.1 us -> 13.1 us
  starting transfers between devices: 31.4 us -> 17.7 us
  between operations: 14 us -> 0.83 us
  other arithmetic: 16.3 us -> 7.6 us
    reduce_scatter x2 -> x0, waiting for transfers between devices: 191 us -> none  [the longest x1 114 us: on_device(): lax.psum_scatter(out_grad, 'dp', scatter_dimension=0, tiled=True)]
    all_gather x3 -> x0, waiting for transfers between devices: 143 us -> none  [the longest x1 67.4 us: on_device(): lax.all_gather(w_out, 'dp', axis=1, tiled=True)]
    all_to_all x4 -> x2, waiting for transfers between devices: 105 us -> 25.1 us  [the longest x1 15.3 us: on_device(): lax.all_to_all(summed.astype(jnp.bfloat16).reshape(blocks, half, model_wi...]
    all_to_all x0 -> x1, blocking collectives: none -> 40.2 us  [dispatch(): lax.all_to_all(sent, everyone, split_axis=0, concat_axis=0, tiled=True)]
    all_to_all x4 -> x2, starting transfers between devices: 24.5 us -> 9.7 us  [the longest x1 4.89 us: dispatch(): lax.all_to_all(sent, everyone, split_axis=0, concat_axis=0, tiled=True)]
    scatter x1 -> x0, local copies, waits for them, and re-layouts: 11.2 us -> none  [slot_table(): slot_index.at[flat_ids, position]]
    gather x5 -> x0, local copies, waits for them, and re-layouts: 9.67 us -> none  [the longest x2 4.45 us: fill_slots(): return padded[slot_index // 2]]
    reshape x2 -> x0, other arithmetic: 6.64 us -> none  [the longest x1 4.02 us: on_device(): w_out_grad = out_share.astype(jnp.bfloat16).reshape(w_out.shape)]
  transfers between devices with their start and end apart: 10 -> 6, of which waited for: 8 -> 3; matrix products, arithmetic and copies ran while one was open for 14% -> 30% of each run, Pallas kernels for 0% -> 0%
where the time goes in v1:
time: 142 us
  blocking collectives  40.2 us (28%)
  matrix products  31.5 us (22%)
  waiting for transfers between devices  31.1 us (22%)
  starting transfers between devices  17.7 us (12%)
  local copies, waits for them, and re-layouts  13.1 us (9%)
  other arithmetic  7.6 us (5%)
    all_to_all x1, blocking collectives, dispatch(): lax.all_to_all(sent, everyone, split_axis=0, concat_axis=0, tiled=True)  40.2 us
    all_to_all x1, waiting for transfers between devices, on_device(): lax.all_to_all(summed.astype(jnp.bfloat16).reshape(blocks, half, model_wi...  15.3 us
    all_to_all x1, waiting for transfers between devices, dispatch(): lax.all_to_all(sent, everyone, split_axis=0, concat_axis=0, tiled=True)  9.81 us
    dot_general x1, matrix products, on_device(): jnp.einsum('rd,rh->dh', input_rows, pre_grad, preferred_element_type=jnp....  8.54 us
    dot_general x1, matrix products, on_device(): jnp.einsum('rd,hd->rh', grad_rows, wout, preferred_element_type=jnp.float32)  8.46 us
    dot_general x1, matrix products, on_device(): jnp.einsum('rh,rd->hd', active.astype(jnp.bfloat16), grad_rows, preferred...  8.33 us
    unnamed x15, local copies, waits for them, and re-layouts  6.7 us
    ppermute x1, starting transfers between devices, on_device(): lax.ppermute(handoff, 'pipe', [(s, (s - 1) % pipe_count) for s in range(p...  6.47 us
  transfers between devices with their start and end apart: 6, of which 3 were waited for; matrix products, arithmetic and copies ran while one was open for 30% of the time, Pallas kernels for 0%

profile of v1, /device:TPU:1, one launch (start us, length us, event | category | flops | bytes accessed | tf_op | source)
XLA Modules:
  0.0 141.9 jit_solution(5621983882972729903)
XLA Ops:
  0.6 6.5 %collective-permute-start = (bf16[1,128,1536]{2,1,0:T(8,128)(2,1)}, bf16[1,128,1536]{2,1,0:T(8,128)(2,1)S(1)}, u32[]{:S(2)}, u32[]{:S(2)}) collective-permute-start(bf16[1,128,1536]{2,1,0:T(8,128)(2,1)} %param.8), channel_id=1, source_target_pairs={{0,224},{32,0},{64,32},{96,64},{128,96},{160,128},{192,160},{224,1... | collective-permute-start | bytes 1179656 | tf_op jit(solution)/shard_map/ppermute | solution.py:42
  7.1 0.8 copy.14
  8.5 0.7 slice_bitcast_fusion.1
  9.3 6.0 %collective-permute-done = bf16[1,128,1536]{2,1,0:T(8,128)(2,1)S(1)} collective-permute-done((bf16[1,128,1536]{2,1,0:T(8,128)(2,1)}, bf16[1,128,1536]{2,1,0:T(8,128)(2,1)S(1)}, u32[]{:S(2)}, u32[]{:S(2)}) %collective-permute-start) | collective-permute-done | bytes 393248 | tf_op jit(solution)/shard_map/ppermute | solution.py:42
  15.9 40.2 %all_to_all.15 = bf16[32,24,1536]{2,1,0:T(8,128)(2,1)} all-to-all(bf16[32,24,1536]{2,1,0:T(8,128)(2,1)S(1)} %bitcast.50), channel_id=1, replica_groups=mesh['pipe'=8,'dp'=2,'expert'=16] {'dp','expert'}, dimensions={0} | all-to-all | bytes 4718592 | tf_op jit(solution)/shard_map/all_to_all | solution.py:63
  56.5 1.6 %broadcast_in_dim.51 = bf16[2,16,24,1536]{3,2,1,0:T(8,128)(2,1)} broadcast(bf16[16,24,1536]{2,1,0:T(8,128)(2,1)S(1)} %bitcast.53), dimensions={1,2,3} | broadcast | bytes 3538944 | tf_op jit(solution)/shard_map/broadcast_in_dim | solution.py:61
  58.1 4.9 %all-to-all-start.2 = ((bf16[32,24,1536]{2,1,0:T(8,128)(2,1)}), bf16[32,24,1536]{2,1,0:T(8,128)(2,1)}, u32[]{:S(2)}, u32[]{:S(2)}) async-start(bf16[32,24,1536]{2,1,0:T(8,128)(2,1)} %bitcast.49), calls=%async_computation.2 | async-start | bytes 4718592 | tf_op jit(solution)/shard_map/all_to_all | solution.py:63
  63.0 1.8 %dynamic-slice_bitcast_fusion.1 = (bf16[32,24,768]{2,1,0:T(8,128)(2,1)S(1)}, bf16[32,24,768]{2,1,0:T(8,128)(2,1)S(1)}) fusion(bf16[32,2,24,768]{3,2,1,0:T(8,128)(2,1)} %bitcast.54, s32[]{:T(128)S(6)} %select_n.24, s32[]{:T(128)S(6)} %select_n.25), kind=kLoop, calls=%fused_computation.42 | loop fusion | bytes 4718600 | tf_op jit(solution)/shard_map/jit(dynamic_index_in_dim)/squeeze | solution.py:78
  65.0 1.4 copy-done.2
  66.4 0.9 copy-done.5
  67.3 8.5 %fusion.9 = bf16[1536,768]{1,0:T(8,128)(2,1)S(1)} fusion(bf16[1536,768]{1,0:T(8,128)(2,1)S(1)} %bitcast.55, bf16[768,1536]{1,0:T(8,128)(2,1)} %bitcast.8, bf16[768,1536]{1,0:T(8,128)(2,1)} %bitcast.7, bf16[1,1,1,768,1536]{4,3,2,1,0:T(8,128)(2,1)S(1)} %copy-done.5), kind=kOutput, calls=%fused_computation.13 | convolution fusion | flops 3655729152 | bytes 11796480 | tf_op jit(solution)/shard_map/rd,hd->rh/dot_general | solution.py:84
  75.8 4.0 %fusion.26 = f32[1536,1536]{1,0:T(8,128)S(1)} fusion(bf16[1536,768]{1,0:T(8,128)(2,1)S(1)} %fusion.9, bf16[1,1536,1,1,768]{4,1,3,2,0:T(8,128)(2,1)S(1)} %copy-done), kind=kOutput, calls=%fused_computation.34 | convolution fusion | flops 3623878656 | bytes 14155776 | tf_op jit(solution)/shard_map/rh,dh->rd/dot_general | solution.py:87
  79.9 3.6 %copy-done.1 = f32[1536,1536]{1,0:T(8,128)} copy-done((f32[1536,1536]{1,0:T(8,128)}, f32[1536,1536]{1,0:T(8,128)S(1)}, u32[]{:S(2)}) %copy-start.1) | copy-done | bytes 9437208
  83.5 1.7 %slice.37 = bf16[768,1536]{1,0:T(8,128)(2,1)} slice(f32[1536,1536]{1,0:T(8,128)S(1)} %fusion.26), slice={[768:1536], [0:1536]} | slice | bytes 4718592 | tf_op jit(solution)/shard_map/slice | solution.py:90
  85.2 0.6 collective-permute-start.2
  85.7 9.8 %all-to-all-done.2 = bf16[32,24,1536]{2,1,0:T(8,128)(2,1)} async-done(((bf16[32,24,1536]{2,1,0:T(8,128)(2,1)}), bf16[32,24,1536]{2,1,0:T(8,128)(2,1)}, u32[]{:S(2)}, u32[]{:S(2)}) %all-to-all-start.2) | async-done | bytes 2359328 | tf_op jit(solution)/shard_map/all_to_all | solution.py:63
  95.5 1.0 collective-permute-start.3
  96.5 5.2 %fusion.13 = bf16[768,1536]{1,0:T(8,128)(2,1)} fusion(f32[1536,1536]{1,0:T(8,128)} %copy-done.1, bf16[768,1536]{1,0:T(8,128)(2,1)} %collective-permute-done.2), kind=kLoop, calls=%fused_computation.19 | loop fusion | flops 3538944 | bytes 9437184 | tf_op jit(solution)/shard_map/convert_element_type | solution.py:93
  101.7 4.8 %all-to-all-start.1 = ((bf16[32,24,1536]{2,1,0:T(8,128)(2,1)}), bf16[32,24,1536]{2,1,0:T(8,128)(2,1)}, u32[]{:S(2)}, u32[]{:S(2)}) async-start(bf16[32,24,1536]{2,1,0:T(8,128)(2,1)} %bitcast.51), calls=%async_computation.1 | async-start | bytes 4718592 | tf_op jit(solution)/shard_map/all_to_all | solution.py:92
  106.6 8.5 %fusion.22 = bf16[1,1536,1,1,768]{4,1,3,2,0:T(8,128)(2,1)} fusion(bf16[1536,768]{1,0:T(8,128)(2,1)} %copy-done.6, bf16[768,1536]{1,0:T(8,128)(2,1)} %bitcast.23, bf16[768,1536]{1,0:T(8,128)(2,1)} %bitcast.22), kind=kOutput, calls=%fused_computation.30 | convolution fusion | flops 3634495488 | bytes 9437184 | tf_op jit(solution)/shard_map/rd,rh->dh/dot_general | solution.py:102
  115.1 8.3 %fusion.21 = bf16[1,1,1,768,1536]{4,3,2,1,0:T(8,128)(2,1)} fusion(bf16[768,1536]{1,0:T(8,128)(2,1)} %bitcast.8, bf16[768,1536]{1,0:T(8,128)(2,1)} %bitcast.7, bf16[1536,768]{1,0:T(8,128)(2,1)S(1)} %bitcast.56), kind=kOutput, calls=%fused_computation.29 | convolution fusion | flops 3646291968 | bytes 9437184 | tf_op jit(solution)/shard_map/rh,rd->hd/dot_general | solution.py:99
  123.4 15.3 %all-to-all-done.1 = bf16[32,24,1536]{2,1,0:T(8,128)(2,1)} async-done(((bf16[32,24,1536]{2,1,0:T(8,128)(2,1)}), bf16[32,24,1536]{2,1,0:T(8,128)(2,1)}, u32[]{:S(2)}, u32[]{:S(2)}) %all-to-all-start.1) | async-done | bytes 2359328 | tf_op jit(solution)/shard_map/all_to_all | solution.py:92
  138.7 2.0 %convert_reduce_fusion = bf16[384,1536]{1,0:T(8,128)(2,1)S(1)} fusion(bf16[2,384,1536]{2,1,0:T(8,128)(2,1)} %bitcast.48), kind=kLoop, calls=%fused_computation.25 | loop fusion | flops 1769472 | bytes 3538944 | tf_op jit(solution)/shard_map/st,psd->td/reduce_sum | solution.py:105
  140.8 1.2 fusion.33
  (24 shorter events, 1.9 us)
Async XLA Ops:
  0.6 75.1 %copy-start = (bf16[1,1536,1,1,768]{4,1,3,2,0:T(8,128)(2,1)S(1)}, bf16[1,1536,1,1,768]{4,1,3,2,0:T(8,128)(2,1)}, u32[]{:S(2)}) copy-start(bf16[1,1536,1,1,768]{4,1,3,2,0:T(8,128)(2,1)} %param.12) | copy-start | bytes 7077892
  0.6 14.6 %collective-permute-start = (bf16[1,128,1536]{2,1,0:T(8,128)(2,1)}, bf16[1,128,1536]{2,1,0:T(8,128)(2,1)S(1)}, u32[]{:S(2)}, u32[]{:S(2)}) collective-permute-start(bf16[1,128,1536]{2,1,0:T(8,128)(2,1)} %param.8), channel_id=1, source_target_pairs={{0,224},{32,0},{64,32},{96,64},{128,96},{160,128},{192,160},{224,1... | collective-permute-start | bytes 1179656 | tf_op jit(solution)/shard_map/ppermute | solution.py:42
  15.9 40.2 %copy-start.4 = (bf16[1,128,1536]{2,1,0:T(8,128)(2,1)S(1)}, bf16[1,128,1536]{2,1,0:T(8,128)(2,1)}, u32[]{:S(2)}) copy-start(bf16[1,128,1536]{2,1,0:T(8,128)(2,1)} %param.7) | copy-start | bytes 1179652
  56.0 9.0 %collective-permute-start.1 = (bf16[32,24,1536]{2,1,0:T(8,128)(2,1)}, bf16[32,24,1536]{2,1,0:T(8,128)(2,1)}, u32[]{:S(2)}, u32[]{:S(2)}) collective-permute-start(bf16[32,24,1536]{2,1,0:T(8,128)(2,1)} %all_to_all.15), channel_id=1, source_target_pairs={{0,1},{1,0},{2,3},{3,2},{4,5},{5,4},{6,7},{7,6},{8,9},{9,8},{10,11... | collective-permute-start | bytes 7077896 | tf_op jit(solution)/shard_map/ppermute | solution.py:68
  58.1 37.5 %all-to-all-start.2 = ((bf16[32,24,1536]{2,1,0:T(8,128)(2,1)}), bf16[32,24,1536]{2,1,0:T(8,128)(2,1)}, u32[]{:S(2)}, u32[]{:S(2)}) async-start(bf16[32,24,1536]{2,1,0:T(8,128)(2,1)} %bitcast.49), calls=%async_computation.2 | async-start | bytes 4718592 | tf_op jit(solution)/shard_map/all_to_all | solution.py:63
  64.8 2.5 %copy-start.5 = (bf16[1,1,1,768,1536]{4,3,2,1,0:T(8,128)(2,1)S(1)}, bf16[1,1,1,768,1536]{4,3,2,1,0:T(8,128)(2,1)}, u32[]{:S(2)}) copy-start(bf16[1,1,1,768,1536]{4,3,2,1,0:T(8,128)(2,1)} %param.13) | copy-start | bytes 7077892
  65.0 1.4 copy-start.2
  75.8 4.1 %copy-start.6 = (bf16[1536,768]{1,0:T(8,128)(2,1)}, bf16[1536,768]{1,0:T(8,128)(2,1)S(1)}, u32[]{:S(2)}) copy-start(bf16[1536,768]{1,0:T(8,128)(2,1)S(1)} %fusion.9) | copy-start | bytes 7077892
  79.8 3.6 %copy-start.1 = (f32[1536,1536]{1,0:T(8,128)}, f32[1536,1536]{1,0:T(8,128)S(1)}, u32[]{:S(2)}) copy-start(f32[1536,1536]{1,0:T(8,128)S(1)} %fusion.26) | copy-start | bytes 28311556
  85.2 11.4 %collective-permute-start.2 = (bf16[768,1536]{1,0:T(8,128)(2,1)}, bf16[768,1536]{1,0:T(8,128)(2,1)}, u32[]{:S(2)}, u32[]{:S(2)}) collective-permute-start(bf16[768,1536]{1,0:T(8,128)(2,1)} %slice.37), channel_id=1, source_target_pairs={{0,1},{1,0},{2,3},{3,2},{4,5},{5,4},{6,7},{7,6},{8,9},{9,8},{10,11... | collective-permute-start | bytes 7077896 | tf_op jit(solution)/shard_map/ppermute | solution.py:91
  95.5 11.0 %collective-permute-start.3 = (bf16[32,24,1536]{2,1,0:T(8,128)(2,1)}, bf16[32,24,1536]{2,1,0:T(8,128)(2,1)}, u32[]{:S(2)}, u32[]{:S(2)}) collective-permute-start(bf16[32,24,1536]{2,1,0:T(8,128)(2,1)} %all-to-all-done.2), channel_id=1, source_target_pairs={{0,1},{1,0},{2,3},{3,2},{4,5},{5,4},{6,7},{7,6},{8,9},{9,8},{10,11... | collective-permute-start | bytes 7077896 | tf_op jit(solution)/shard_map/ppermute | solution.py:68
  101.7 37.0 %all-to-all-start.1 = ((bf16[32,24,1536]{2,1,0:T(8,128)(2,1)}), bf16[32,24,1536]{2,1,0:T(8,128)(2,1)}, u32[]{:S(2)}, u32[]{:S(2)}) async-start(bf16[32,24,1536]{2,1,0:T(8,128)(2,1)} %bitcast.51), calls=%async_computation.1 | async-start | bytes 4718592 | tf_op jit(solution)/shard_map/all_to_all | solution.py:92
  106.6 8.6 %copy-start.3 = (bf16[64,24,768]{2,1,0:T(8,128)(2,1)S(1)}, bf16[64,24,768]{2,1,0:T(8,128)(2,1)}, u32[]{:S(2)}) copy-start(bf16[64,24,768]{2,1,0:T(8,128)(2,1)} %copy-done.2) | copy-start | bytes 7077892

commit v2 on v1

v2 whole, which is shorter than its diff:
```python
import math

import jax
import jax.numpy as jnp
import numpy as np
from jax import lax
from jax.experimental import pallas as pl
from jax.experimental.pallas import tpu as pltpu
from jax.sharding import PartitionSpec as P

root_two_pi = math.sqrt(2.0 / math.pi)
cubic_coef = 0.044715
SIDE = 4
ARRIVAL = (1, 3, 2)
TURN = (0, 2, 3, 1)
TILE = 256
WIDE = 256
SPAN = 256


def gelu_parts(values):
    square = values * values
    tangent = jnp.tanh(root_two_pi * values * (1.0 + cubic_coef * square))
    half = 0.5 * (1.0 + tangent)
    slope = half + 0.5 * values * (1.0 - tangent * tangent) * root_two_pi * (
        1.0 + 3.0 * cubic_coef * square
    )
    return (values * half, slope)


def place(x, y, core):
    return (y % 2) * (SIDE * SIDE) + (y // 2) * (2 * SIDE) + x * 2 + core


def send(value, x_core, x_steps, y_steps):
    pairs = []
    for x in range(SIDE):
        for y in range(SIDE):
            for core in range(2):
                to_x = (x + x_steps) % SIDE if core == x_core else x
                to_y = y if core == x_core else (y + y_steps) % SIDE
                pairs.append((place(x, y, core), place(to_x, to_y, core)))
    return lax.ppermute(value, ("dp", "expert"), pairs)


def send_second(value, k):
    return send(value, 1, TURN[k], k)


def send_back(value, k):
    return send(value, 1, -TURN[k], -k)


def swap_cores(value):
    count = lax.axis_size("expert")
    return lax.ppermute(value, "expert", [(e, e ^ 1) for e in range(count)])


def first_stage(value):
    return [value] + [send(value, 0, k, k) for k in range(1, SIDE)]


def weight_grad(left, right):
    height, width = left[0].shape[1], right[0].shape[1]

    def body(*refs):
        lefts, rights, out_ref = refs[: len(left)], refs[len(left) : -1], refs[-1]
        across = width // WIDE

        def tile(i, carry):
            here = pl.ds(pl.multiple_of(i // across * TILE, TILE), TILE)
            there = pl.ds(pl.multiple_of(i % across * WIDE, WIDE), WIDE)
            tall = jnp.concatenate([ref[:, here] for ref in lefts], axis=0)
            flat = jnp.concatenate([ref[:, there] for ref in rights], axis=0)
            out_ref[here, there] = lax.dot_general(
                tall, flat, (((0,), (0,)), ((), ())), preferred_element_type=jnp.float32
            ).astype(jnp.bfloat16)
            return carry

        lax.fori_loop(0, height // TILE * across, tile, 0)

    held = pl.BlockSpec(memory_space=pltpu.VMEM)
    return pl.pallas_call(
        body,
        out_shape=jax.ShapeDtypeStruct((height, width), jnp.bfloat16),
        in_specs=[held] * (len(left) + len(right)),
        out_specs=held,
        compiler_params=pltpu.CompilerParams(vmem_limit_bytes=24 << 20),
    )(*left, *right)


def make_tags(choices, gates, capacity, expert_total):
    token_total = choices.shape[1]

    def body(choice_ref, gate_ref, out_ref):
        experts = lax.broadcasted_iota(jnp.int32, (expert_total, token_total), 0)
        picked = [experts == choice_ref[k : k + 1, :] for k in range(2)]
        named = jnp.where(picked[0] | picked[1], 1.0, 0.0).astype(jnp.bfloat16)
        row = lax.broadcasted_iota(jnp.int32, (token_total, token_total), 0)
        column = lax.broadcasted_iota(jnp.int32, (token_total, token_total), 1)
        earlier = jnp.where(row < column, 1.0, 0.0).astype(jnp.bfloat16)
        counts = jnp.dot(named, earlier, preferred_element_type=jnp.float32)
        starts = (experts * capacity).astype(jnp.float32)
        for k in range(2):
            out_ref[k : k + 1, :] = jnp.sum(
                jnp.where(picked[k], starts + counts, 0.0), axis=0, keepdims=True
            )
        out_ref[2:4, :] = gate_ref[...].astype(jnp.float32)

    held = pl.BlockSpec(memory_space=pltpu.VMEM)
    return pl.pallas_call(
        body,
        out_shape=jax.ShapeDtypeStruct((4, token_total), jnp.float32),
        in_specs=[held, held],
        out_specs=held,
        compiler_params=pltpu.CompilerParams(vmem_limit_bytes=4 << 20),
        name="tags",
    )(choices, gates)


def order_table():
    table = np.zeros((2 * SIDE * SIDE, SIDE + 2 * SIDE * SIDE), np.int32)
    for x in range(SIDE):
        for y in range(SIDE):
            for core in range(2):
                row = table[place(x, y, core)]
                for k in range(SIDE):
                    to_x = x if core == 0 else (x + TURN[k]) % SIDE
                    to_y = (y + k) % SIDE if core == 0 else y
                    row[k] = (to_y // 2) * SIDE + to_x
                    for j in range(SIDE):
                        at = SIDE + k * SIDE + j
                        by_y = place((x - j) % SIDE, (y - k) % SIDE, 0)
                        by_x = place((x - TURN[k]) % SIDE, (y - j) % SIDE, 1)
                        row[at] = by_x if core else by_y
                        row[at + SIDE * SIDE] = by_y if core else by_x
    return table


def selector(experts_ref, tag_ref, capacity, gated):
    token_total = tag_ref.shape[1]
    slot = lax.broadcasted_iota(jnp.int32, (capacity, token_total), 0)
    keys = tag_ref[0:2, :].astype(jnp.int32)
    gates = tag_ref[2:4, :] if gated else jnp.ones((2, token_total), jnp.float32)
    pieces = []
    for k in range(SIDE):
        local = keys - experts_ref[k] * capacity
        pieces.append(
            jnp.where(slot == local[0:1, :], gates[0:1, :], 0.0)
            + jnp.where(slot == local[1:2, :], gates[1:2, :], 0.0)
        )
    return jnp.concatenate(pieces, axis=0).astype(jnp.bfloat16)


def held_call(body, out_shape, experts, operands):
    held = pl.BlockSpec(memory_space=pltpu.VMEM)
    return pl.pallas_call(
        body,
        out_shape=out_shape,
        in_specs=[pl.BlockSpec(memory_space=pltpu.SMEM)] + [held] * len(operands),
        out_specs=tuple(held for _ in out_shape),
        compiler_params=pltpu.CompilerParams(vmem_limit_bytes=20 << 20),
    )(experts, *operands)


def pick_slots(experts, tags, tokens, capacity, gated):
    width = tokens[0].shape[1]

    def body(experts_ref, *refs):
        tag_refs, token_refs, out_refs = refs[:SIDE], refs[SIDE : 2 * SIDE], refs[2 * SIDE :]
        selects = [selector(experts_ref, ref, capacity, gated) for ref in tag_refs]

        def columns(i, carry):
            here = pl.ds(pl.multiple_of(i * SPAN, SPAN), SPAN)
            for j in range(SIDE):
                rows = jnp.dot(
                    selects[j], token_refs[j][:, here], preferred_element_type=jnp.float32
                ).astype(jnp.bfloat16)
                for k in range(SIDE):
                    out_refs[k][pl.ds(j * capacity, capacity), here] = rows[
                        k * capacity : (k + 1) * capacity
                    ]
            return carry

        lax.fori_loop(0, width // SPAN, columns, 0)

    shape = jax.ShapeDtypeStruct((SIDE * capacity, width), jnp.bfloat16)
    return held_call(body, (shape,) * SIDE, experts, tuple(tags) + tuple(tokens))


def combine_slots(experts, tags, returned, grad_tokens, capacity):
    token_total, width = grad_tokens.shape

    def body(experts_ref, *refs):
        tag_refs, row_refs = refs[:SIDE], refs[SIDE : 2 * SIDE]
        grad_ref, out_refs = refs[2 * SIDE], refs[2 * SIDE + 1 :]
        selects = [selector(experts_ref, ref, capacity, False) for ref in tag_refs]

        def columns(i, carry):
            here = pl.ds(pl.multiple_of(i * SPAN, SPAN), SPAN)
            for j in range(SIDE):
                rows = jnp.concatenate(
                    [ref[pl.ds(j * capacity, capacity), here] for ref in row_refs], axis=0
                )
                sums = lax.dot_general(
                    selects[j], rows, (((0,), (0,)), ((), ())), preferred_element_type=jnp.float32
                )
                if j == 0:
                    out_refs[0][:, here] = sums + grad_ref[:, here].astype(jnp.float32)
                else:
                    out_refs[j][:, here] = sums.astype(jnp.bfloat16)
            return carry

        lax.fori_loop(0, width // SPAN, columns, 0)

    shapes = [jax.ShapeDtypeStruct((token_total, width), jnp.float32)]
    shapes += [jax.ShapeDtypeStruct((token_total, width), jnp.bfloat16)] * (SIDE - 1)
    return held_call(body, tuple(shapes), experts, tuple(tags) + tuple(returned) + (grad_tokens,))


def section(layer_input, handoff, routes, gating, saved_pre, w_in, w_out):
    pipe_count = lax.axis_size("pipe")
    blocks, capacity, panel_size = saved_pre.shape[3:]
    model_width = w_in.shape[1]
    wide = jnp.float32
    narrow = jnp.bfloat16
    chunk = SIDE * capacity

    dp_index = lax.axis_index("dp")
    expert_index = lax.axis_index("expert")
    device = dp_index * lax.axis_size("expert") + expert_index
    spot = lax.dynamic_index_in_dim(jnp.asarray(order_table()), device, 0, keepdims=False)

    incoming = lax.ppermute(handoff, "pipe", [(s, (s - 1) % pipe_count) for s in range(pipe_count)])
    grad_tokens = incoming[0]
    input_blocks = first_stage(layer_input[0])
    tags = make_tags(routes[0].T, gating[0].T, capacity, lax.axis_size("expert") // 2)
    tag_blocks = first_stage(tags)
    grad_blocks = first_stage(grad_tokens)

    experts, orders = spot[:SIDE], spot[SIDE:]
    grad_own = list(pick_slots(experts, tag_blocks, grad_blocks, capacity, True))
    input_own = list(pick_slots(experts, tag_blocks, input_blocks, capacity, False))
    for k in ARRIVAL:
        grad_own[k] = send_second(grad_own[k], k)
        input_own[k] = send_second(input_own[k], k)
    input_sib = []
    for k in range(SIDE):
        pieces = 1
        rows = chunk // pieces
        for piece in range(pieces):
            input_sib.append(swap_cores(input_own[k][piece * rows : (piece + 1) * rows]))

    pre_blocks = saved_pre.reshape(blocks, capacity, panel_size)
    ordered = pre_blocks.at[orders].get(mode="promise_in_bounds")
    ordered = lax.optimization_barrier(ordered.reshape(2 * SIDE * chunk, panel_size))
    actives = [gelu_parts(ordered.astype(wide))[0].astype(narrow)]
    win = w_in.reshape(model_width, panel_size)
    wout = w_out.reshape(panel_size, model_width)

    def hidden(grad_rows, side, at):
        upstream = jnp.einsum("rd,hd->rh", grad_rows, wout, preferred_element_type=wide)
        values = ordered[(side * SIDE + at) * chunk : (side * SIDE + at + 1) * chunk]
        return (upstream * gelu_parts(values.astype(wide))[1]).astype(narrow)

    def to_model(pre_grad):
        return jnp.einsum("rh,dh->rd", pre_grad, win, preferred_element_type=wide)

    back = [None] * SIDE
    grad_sib = [None] * SIDE
    hidden_own = [None] * SIDE
    hidden_sib = [None] * SIDE
    for k in (0,) + ARRIVAL:
        grad_sib[k] = swap_cores(grad_own[k])
        hidden_own[k] = hidden(grad_own[k], 0, k)
        hidden_sib[k] = hidden(grad_sib[k], 1, k)
        rows_sib = to_model(hidden_sib[k]).astype(narrow)
        theirs = swap_cores(rows_sib)
        part = (to_model(hidden_own[k]) + theirs.astype(wide)).astype(narrow)
        part = send_back(part, k) if k else part
        back[k] = part

    out_grad = weight_grad(actives, grad_own + grad_sib)
    in_grad = weight_grad(input_own + input_sib, hidden_own + hidden_sib)

    partial = combine_slots(experts, tag_blocks, back, grad_tokens, capacity)
    total = partial[0]
    for j in ARRIVAL:
        total = total + send(partial[j], 0, -j, -j).astype(wide)
    return (
        total.astype(narrow)[None],
        in_grad.reshape(w_in.shape),
        out_grad.reshape(w_out.shape),
    )


def solution(mesh):
    in_specs = (
        P("pipe", ("dp", "expert"), None),
        P("pipe", ("dp", "expert"), None),
        P("pipe", ("dp", "expert"), None),
        P("pipe", ("dp", "expert"), None),
        P("pipe", "dp", "expert", None, None, None),
        P("pipe", None, "dp", "expert", None),
        P("pipe", "dp", "expert", None, None),
    )
    out_specs = (
        P("pipe", ("dp", "expert"), None),
        P("pipe", None, "dp", "expert", None),
        P("pipe", "dp", "expert", None, None),
    )
    return jax.shard_map(
        section, mesh=mesh, in_specs=in_specs, out_specs=out_specs, check_vma=False
    )
```

time: 142 us -> 151 us (1.063)
  blocking collectives: 40.2 us -> 0 us
  starting transfers between devices: 17.7 us -> 50.9 us
  Pallas kernels: 0 us -> 28.1 us
  matrix products: 31.5 us -> 18.7 us
  waiting for transfers between devices: 31.1 us -> 39.1 us
  other arithmetic: 7.6 us -> 2.6 us
  local copies, waits for them, and re-layouts: 13.1 us -> 9.98 us
    ppermute x4 -> x34, starting transfers between devices: 8.03 us -> 50.9 us  [the longest x21 33.6 us: send(): return lax.ppermute(value, ('dp', 'expert'), pairs)]
    all_to_all x1 -> x0, blocking collectives: 40.2 us -> none  [dispatch(): lax.all_to_all(sent, everyone, split_axis=0, concat_axis=0, tiled=True)]
    ppermute x4 -> x34, waiting for transfers between devices: 5.98 us -> 39.1 us  [the longest x21 30.9 us: send(): return lax.ppermute(value, ('dp', 'expert'), pairs)]
    pallas_call x0 -> x6, Pallas kernels: none -> 28.1 us  [the longest x2 19.5 us: weight_grad(): pl.pallas_call(body, out_shape=jax.ShapeDtypeStruct((height, width), jnp....]
    all_to_all x2 -> x0, waiting for transfers between devices: 25.1 us -> none  [the longest x1 15.3 us: on_device(): lax.all_to_all(summed.astype(jnp.bfloat16).reshape(blocks, half, model_wi...]
    dot_general x7 -> x16, matrix products: 31.5 us -> 18.7 us  [the longest x8 11.4 us: hidden(): jnp.einsum('rd,hd->rh', grad_rows, wout, preferred_element_type=wide)]
    all_to_all x2 -> x0, starting transfers between devices: 9.7 us -> none  [the longest x1 4.89 us: dispatch(): lax.all_to_all(sent, everyone, split_axis=0, concat_axis=0, tiled=True)]
    convert_element_type x1, other arithmetic: 5.22 us -> 1.6 us  [section(): actives = [gelu_parts(ordered.astype(wide))[0].astype(narrow)]]
  transfers between devices with their start and end apart: 6 -> 34, of which waited for: 3 -> 7; matrix products, arithmetic and copies ran while one was open for 30% -> 15% of each run, Pallas kernels for 0% -> 16%
where the time goes in v2:
time: 151 us; the launch traced here: 150 us
  starting transfers between devices  50.9 us (34%)
  waiting for transfers between devices  39.1 us (26%)
  Pallas kernels  28.1 us (19%)
  matrix products  18.7 us (12%)
  local copies, waits for them, and re-layouts  9.98 us (7%)
  other arithmetic  2.6 us (2%)
    ppermute x21, starting transfers between devices, send(): return lax.ppermute(value, ('dp', 'expert'), pairs)  33.6 us
    ppermute x21, waiting for transfers between devices, send(): return lax.ppermute(value, ('dp', 'expert'), pairs)  30.9 us
    pallas_call x2, Pallas kernels, weight_grad(): pl.pallas_call(body, out_shape=jax.ShapeDtypeStruct((height, width), jnp....  19.5 us
    dot_general x8, matrix products, hidden(): jnp.einsum('rd,hd->rh', grad_rows, wout, preferred_element_type=wide)  11.4 us
    ppermute x12, starting transfers between devices, swap_cores(): return lax.ppermute(value, 'expert', [(e, e ^ 1) for e in range(count)])  10.8 us
    pallas_call x3, Pallas kernels, held_call(): pl.pallas_call(body, out_shape=out_shape, in_specs=[pl.BlockSpec(memory_s...  8.54 us
    ppermute x1, waiting for transfers between devices, section(): lax.ppermute(handoff, 'pipe', [(s, (s - 1) % pipe_count) for s in range(p...  8.11 us
    dot_general x8, matrix products, to_model(): return jnp.einsum('rh,dh->rd', pre_grad, win, preferred_element_type=wide)  7.35 us
  transfers between devices with their start and end apart: 34, of which 7 were waited for; matrix products, arithmetic and copies ran while one was open for 15% of the time, Pallas kernels for 16%

profile of v2, /device:TPU:1, one launch (start us, length us, event | category | flops | bytes accessed | tf_op | source)
XLA Modules:
  0.0 150.3 jit_solution(748454385181463583)
XLA Ops:
  0.6 6.5 %collective-permute-start.3 = (bf16[1,128,1536]{2,1,0:T(8,128)(2,1)}, bf16[1,128,1536]{2,1,0:T(8,128)(2,1)S(1)}, u32[]{:S(2)}, u32[]{:S(2)}) collective-permute-start(bf16[1,128,1536]{2,1,0:T(8,128)(2,1)} %param.9), channel_id=1, source_target_pairs={{0,224},{32,0},{64,32},{96,64},{128,96},{160,128},{192,160},{224,1... | collective-permute-start | bytes 1179656 | tf_op jit(solution)/shard_map/ppermute | solution.py:234
  7.1 8.1 %collective-permute-done.3 = bf16[1,128,1536]{2,1,0:T(8,128)(2,1)S(1)} collective-permute-done((bf16[1,128,1536]{2,1,0:T(8,128)(2,1)}, bf16[1,128,1536]{2,1,0:T(8,128)(2,1)S(1)}, u32[]{:S(2)}, u32[]{:S(2)}) %collective-permute-start.3) | collective-permute-done | bytes 393248 | tf_op jit(solution)/shard_map/ppermute | solution.py:234
  16.5 2.6 %collective-permute-start.5 = (bf16[128,1536]{1,0:T(8,128)(2,1)S(1)}, bf16[128,1536]{1,0:T(8,128)(2,1)S(1)}, u32[]{:S(2)}, u32[]{:S(2)}) collective-permute-start(bf16[128,1536]{1,0:T(8,128)(2,1)S(1)} %bitcast.112), channel_id=1, source_target_pairs={{0,4},{1,9},{16,20},{17,25},{8,12},{9,1},{24,28},{25,17},{2,6},{3,... | collective-permute-start | bytes 1179656 | tf_op jit(solution)/shard_map/ppermute | solution.py:43
  23.6 2.0 %collective-permute-done.refs_1_ = f32[4,128]{1,0:T(4,128)S(1)} collective-permute-done((f32[4,128]{1,0:T(4,128)S(1)}, f32[4,128]{1,0:T(4,128)S(1)}, u32[]{:S(2)}, u32[]{:S(2)}) %collective-permute-start) | collective-permute-done | bytes 2080 | tf_op jit(solution)/shard_map/ppermute | solution.py:43
  25.6 3.7 %collective-permute-start.2 = (f32[4,128]{1,0:T(4,128)S(1)}, f32[4,128]{1,0:T(4,128)S(1)}, u32[]{:S(2)}, u32[]{:S(2)}) collective-permute-start(f32[4,128]{1,0:T(4,128)S(1)} %tags.1.refs_0_), channel_id=1, source_target_pairs={{0,6},{1,25},{16,22},{17,1},{8,14},{9,17},{24,30},{25,9},{2,0},{3,... | collective-permute-start | bytes 6152 | tf_op jit(solution)/shard_map/ppermute | solution.py:43
  33.5 3.4 %shard_map.103 = (bf16[192,1536]{1,0:T(8,128)(2,1)S(1)}, bf16[192,1536]{1,0:T(8,128)(2,1)S(1)}, bf16[192,1536]{1,0:T(8,128)(2,1)}, bf16[192,1536]{1,0:T(8,128)(2,1)S(1)}) custom-call(s32[4]{0:T(128)S(1)} %slice_bitcast_fusion.experts_ref, f32[4,128]{1,0:T(4,128)S(1)} %tags.1.refs_0_, f32[4,128]{1,0:T(4,128)S(1)} %collective-permute-done.refs_1_, ...), custom_call_target="tpu_custom_call" | custom-call | tf_op jit(solution)/shard_map/pallas_call | solution.py:157
  38.2 2.9 %collective-permute-start.7 = (bf16[192,1536]{1,0:T(8,128)(2,1)S(1)}, bf16[192,1536]{1,0:T(8,128)(2,1)}, u32[]{:S(2)}, u32[]{:S(2)}) collective-permute-start(bf16[192,1536]{1,0:T(8,128)(2,1)S(1)} %get-tuple-element.15.refs_1_), channel_id=1, source_target_pairs={{0,1},{1,0},{2,3},{3,2},{4,5},{5,4},{6,7},{7,6},{8,9},{9,8},{10,11... | collective-permute-start | bytes 1769480 | tf_op jit(solution)/shard_map/ppermute | solution.py:56
  42.4 2.6 %collective-permute-start.25 = (bf16[128,1536]{1,0:T(8,128)(2,1)}, bf16[128,1536]{1,0:T(8,128)(2,1)}, u32[]{:S(2)}, u32[]{:S(2)}) collective-permute-start(bf16[128,1536]{1,0:T(8,128)(2,1)} %bitcast.117), channel_id=1, source_target_pairs={{0,4},{1,9},{16,20},{17,25},{8,12},{9,1},{24,28},{25,17},{2,6},{3,... | collective-permute-start | bytes 1179656 | tf_op jit(solution)/shard_map/ppermute | solution.py:43
  46.1 3.2 %collective-permute-start.13 = (bf16[192,1536]{1,0:T(8,128)(2,1)}, bf16[192,1536]{1,0:T(8,128)(2,1)}, u32[]{:S(2)}, u32[]{:S(2)}) collective-permute-start(bf16[192,1536]{1,0:T(8,128)(2,1)} %get-tuple-element.17), channel_id=1, source_target_pairs={{0,8},{1,7},{16,24},{17,23},{8,0},{9,15},{24,16},{25,31},{2,10},{3... | collective-permute-start | bytes 1769480 | tf_op jit(solution)/shard_map/ppermute | solution.py:43
  49.4 2.1 %gather_fusion = bf16[32,48,768]{2,1,0:T(8,128)(2,1)} fusion(bf16[32,48,768]{2,1,0:T(8,128)(2,1)S(1)} %bitcast.110, s32[1024]{0:T(1024)S(1)} %pad_clamp_fusion), kind=kCustom, calls=%fused_computation | custom fusion | bytes 4718720 | tf_op jit(solution)/shard_map/gather | solution.py:255
  51.5 7.5 %collective-permute-done.25.refs_6_ = bf16[128,1536]{1,0:T(8,128)(2,1)} collective-permute-done((bf16[128,1536]{1,0:T(8,128)(2,1)}, bf16[128,1536]{1,0:T(8,128)(2,1)}, u32[]{:S(2)}, u32[]{:S(2)}) %collective-permute-start.25) | collective-permute-done | bytes 393248 | tf_op jit(solution)/shard_map/ppermute | solution.py:43
  60.0 2.8 %shard_map.105 = (bf16[192,1536]{1,0:T(8,128)(2,1)S(1)}, bf16[192,1536]{1,0:T(8,128)(2,1)S(1)}, bf16[192,1536]{1,0:T(8,128)(2,1)S(1)}, bf16[192,1536]{1,0:T(8,128)(2,1)S(1)}) custom-call(s32[4]{0:T(128)S(1)} %copy-done.7, f32[4,128]{1,0:T(4,128)S(1)} %tags.1.refs_0_, f32[4,128]{1,0:T(4,128)S(1)} %collective-permute-done.refs_1_, ...), custom_call_target="tpu_custom_call" | custom-call | tf_op jit(solution)/shard_map/pallas_call | solution.py:157
  64.5 3.8 %collective-permute-start.28 = (bf16[192,1536]{1,0:T(8,128)(2,1)S(1)}, bf16[192,1536]{1,0:T(8,128)(2,1)S(1)}, u32[]{:S(2)}, u32[]{:S(2)}) collective-permute-start(bf16[192,1536]{1,0:T(8,128)(2,1)S(1)} %get-tuple-element.25), channel_id=1, source_target_pairs={{0,8},{1,7},{16,24},{17,23},{8,0},{9,15},{24,16},{25,31},{2,10},{3... | collective-permute-start | bytes 1769480 | tf_op jit(solution)/shard_map/ppermute | solution.py:43
  68.8 2.1 %collective-permute-start.9 = (bf16[192,1536]{1,0:T(8,128)(2,1)}, bf16[192,1536]{1,0:T(8,128)(2,1)S(1)}, u32[]{:S(2)}, u32[]{:S(2)}) collective-permute-start(bf16[192,1536]{1,0:T(8,128)(2,1)} %copy-done.12), channel_id=1, source_target_pairs={{0,16},{1,5},{16,8},{17,21},{8,24},{9,13},{24,0},{25,29},{2,18},{3... | collective-permute-start | bytes 1769480 | tf_op jit(solution)/shard_map/ppermute | solution.py:43
  70.8 2.9 %fusion.77.refs_12_ = bf16[192,768]{1,0:T(8,128)(2,1)S(1)} fusion(bf16[192,1536]{1,0:T(8,128)(2,1)} %collective-permute-done.7.refs_5_, bf16[1,1,1,768,1536]{4,3,2,1,0:T(8,128)(2,1)} %param.14, bf16[1536,768]{1,0:T(8,128)(2,1)} %bitcast.122), kind=kOutput, calls=%fused_computation.57 | convolution fusion | flops 455786496 | bytes 3538944 | tf_op jit(solution)/shard_map/rd,hd->rh/dot_general | solution.py:262
  74.8 2.1 %fusion.68.refs_10_ = bf16[192,768]{1,0:T(8,128)(2,1)S(1)} fusion(bf16[192,1536]{1,0:T(8,128)(2,1)} %collective-permute-done.13.refs_3_, bf16[1,1,1,768,1536]{4,3,2,1,0:T(8,128)(2,1)S(1)} %copy-done.15, bf16[1536,768]{1,0:T(8,128)(2,1)S(1)} %bitcast.123), kind=kOutput, calls=%fused_computation.54 | convolution fusion | flops 455786496 | bytes 3538944 | tf_op jit(solution)/shard_map/rd,hd->rh/dot_general | solution.py:262
  76.9 8.9 %collective-permute-done.9.refs_2_ = bf16[192,1536]{1,0:T(8,128)(2,1)S(1)} collective-permute-done((bf16[192,1536]{1,0:T(8,128)(2,1)}, bf16[192,1536]{1,0:T(8,128)(2,1)S(1)}, u32[]{:S(2)}, u32[]{:S(2)}) %collective-permute-start.9) | collective-permute-done | bytes 589856 | tf_op jit(solution)/shard_map/ppermute | solution.py:43
  85.9 3.9 %collective-permute-start.14 = (bf16[192,1536]{1,0:T(8,128)(2,1)}, bf16[192,1536]{1,0:T(8,128)(2,1)S(1)}, u32[]{:S(2)}, u32[]{:S(2)}) collective-permute-start(bf16[192,1536]{1,0:T(8,128)(2,1)} %collective-permute-done.13.refs_3_), channel_id=1, source_target_pairs={{0,1},{1,0},{2,3},{3,2},{4,5},{5,4},{6,7},{7,6},{8,9},{9,8},{10,11... | collective-permute-start | bytes 1769480 | tf_op jit(solution)/shard_map/ppermute | solution.py:56
  105.0 2.5 %collective-permute-start.20 = (bf16[192,1536]{1,0:T(8,128)(2,1)S(1)}, bf16[192,1536]{1,0:T(8,128)(2,1)S(1)}, u32[]{:S(2)}, u32[]{:S(2)}) collective-permute-start(bf16[192,1536]{1,0:T(8,128)(2,1)S(1)} %add_convert_fusion), channel_id=1, source_target_pairs={{0,16},{1,7},{16,8},{17,23},{8,24},{9,15},{24,0},{25,31},{2,18},{3... | collective-permute-start | bytes 1769480 | tf_op jit(solution)/shard_map/ppermute | solution.py:43
  109.9 11.5 %collective-permute-done.16.refs_6_ = bf16[192,1536]{1,0:T(8,128)(2,1)S(1)} collective-permute-done((bf16[192,1536]{1,0:T(8,128)(2,1)S(1)}, bf16[192,1536]{1,0:T(8,128)(2,1)S(1)}, u32[]{:S(2)}, u32[]{:S(2)}) %collective-permute-start.16) | collective-permute-done | bytes 589856 | tf_op jit(solution)/shard_map/ppermute | solution.py:43
  122.6 2.3 %shard_map.104 = (f32[128,1536]{1,0:T(8,128)S(1)}, bf16[128,1536]{1,0:T(8,128)(2,1)S(1)}, bf16[128,1536]{1,0:T(8,128)(2,1)S(1)}, bf16[128,1536]{1,0:T(8,128)(2,1)S(1)}) custom-call(s32[4]{0:T(128)S(1)} %copy-done.7, f32[4,128]{1,0:T(4,128)S(1)} %tags.1.refs_0_, f32[4,128]{1,0:T(4,128)S(1)} %collective-permute-done.refs_1_, ...), custom_call_target="tpu_custom_call" | custom-call | tf_op jit(solution)/shard_map/pallas_call | solution.py:157
  126.5 1.8 %collective-permute-start.23 = (bf16[128,1536]{1,0:T(8,128)(2,1)S(1)}, bf16[128,1536]{1,0:T(8,128)(2,1)S(1)}, u32[]{:S(2)}, u32[]{:S(2)}) collective-permute-start(bf16[128,1536]{1,0:T(8,128)(2,1)S(1)} %get-tuple-element.22), channel_id=1, source_target_pairs={{0,4},{1,9},{16,20},{17,25},{8,12},{9,1},{24,28},{25,17},{2,6},{3,... | collective-permute-start | bytes 1179656 | tf_op jit(solution)/shard_map/ppermute | solution.py:43
  129.9 10.3 %shard_map.107 = bf16[768,1536]{1,0:T(8,128)(2,1)} custom-call(bf16[1536,768]{1,0:T(8,128)(2,1)S(1)} %fusion.6.refs_0_, bf16[192,1536]{1,0:T(8,128)(2,1)S(1)} %get-tuple-element.15.refs_1_, bf16[192,1536]{1,0:T(8,128)(2,1)S(1)} %collective-permute-done.9.refs_2_, bf16[192,1536]{1,0:T(8,128)(2,1)} %collective-permute-done.13.refs_3_, ...), custom_call_target="tpu_custom_call" | custom-call | tf_op jit(solution)/shard_map/pallas_call | solution.py:83
  140.2 9.2 %shard_map.106 = bf16[1536,768]{1,0:T(8,128)(2,1)} custom-call(bf16[192,1536]{1,0:T(8,128)(2,1)S(1)} %get-tuple-element.23.refs_0_, bf16[192,1536]{1,0:T(8,128)(2,1)S(1)} %collective-permute-done.27.refs_1_, bf16[192,1536]{1,0:T(8,128)(2,1)S(1)} %collective-permute-done.28.refs_2_, bf16[192,1536]{1,0:T(8,128)(2,1)S(1)} %collective-permute-done.29.refs_3_, ...), custom_call_target="tpu_custom_call" | custom-call | tf_op jit(solution)/shard_map/pallas_call | solution.py:83
  (105 shorter events, 40.8 us)
Async XLA Ops:
  0.6 14.6 %collective-permute-start.3 = (bf16[1,128,1536]{2,1,0:T(8,128)(2,1)}, bf16[1,128,1536]{2,1,0:T(8,128)(2,1)S(1)}, u32[]{:S(2)}, u32[]{:S(2)}) collective-permute-start(bf16[1,128,1536]{2,1,0:T(8,128)(2,1)} %param.9), channel_id=1, source_target_pairs={{0,224},{32,0},{64,32},{96,64},{128,96},{160,128},{192,160},{224,1... | collective-permute-start | bytes 1179656 | tf_op jit(solution)/shard_map/ppermute | solution.py:234
  15.2 14.7 %collective-permute-start.4 = (bf16[128,1536]{1,0:T(8,128)(2,1)S(1)}, bf16[128,1536]{1,0:T(8,128)(2,1)S(1)}, u32[]{:S(2)}, u32[]{:S(2)}) collective-permute-start(bf16[128,1536]{1,0:T(8,128)(2,1)S(1)} %bitcast.111), channel_id=1, source_target_pairs={{0,2},{1,17},{16,18},{17,9},{8,10},{9,25},{24,26},{25,1},{2,4},{3,... | collective-permute-start | bytes 1179656 | tf_op jit(solution)/shard_map/ppermute | solution.py:43
  16.5 14.2 %collective-permute-start.5 = (bf16[128,1536]{1,0:T(8,128)(2,1)S(1)}, bf16[128,1536]{1,0:T(8,128)(2,1)S(1)}, u32[]{:S(2)}, u32[]{:S(2)}) collective-permute-start(bf16[128,1536]{1,0:T(8,128)(2,1)S(1)} %bitcast.112), channel_id=1, source_target_pairs={{0,4},{1,9},{16,20},{17,25},{8,12},{9,1},{24,28},{25,17},{2,6},{3,... | collective-permute-start | bytes 1179656 | tf_op jit(solution)/shard_map/ppermute | solution.py:43
  19.2 12.3 %collective-permute-start.6 = (bf16[128,1536]{1,0:T(8,128)(2,1)S(1)}, bf16[128,1536]{1,0:T(8,128)(2,1)}, u32[]{:S(2)}, u32[]{:S(2)}) collective-permute-start(bf16[128,1536]{1,0:T(8,128)(2,1)S(1)} %bitcast.113), channel_id=1, source_target_pairs={{0,6},{1,25},{16,22},{17,1},{8,14},{9,17},{24,30},{25,9},{2,0},{3,... | collective-permute-start | bytes 1179656 | tf_op jit(solution)/shard_map/ppermute | solution.py:43
  38.2 30.5 %collective-permute-start.7 = (bf16[192,1536]{1,0:T(8,128)(2,1)S(1)}, bf16[192,1536]{1,0:T(8,128)(2,1)}, u32[]{:S(2)}, u32[]{:S(2)}) collective-permute-start(bf16[192,1536]{1,0:T(8,128)(2,1)S(1)} %get-tuple-element.15.refs_1_), channel_id=1, source_target_pairs={{0,1},{1,0},{2,3},{3,2},{4,5},{5,4},{6,7},{7,6},{8,9},{9,8},{10,11... | collective-permute-start | bytes 1769480 | tf_op jit(solution)/shard_map/ppermute | solution.py:56
  41.1 10.4 %collective-permute-start.24 = (bf16[128,1536]{1,0:T(8,128)(2,1)}, bf16[128,1536]{1,0:T(8,128)(2,1)}, u32[]{:S(2)}, u32[]{:S(2)}) collective-permute-start(bf16[128,1536]{1,0:T(8,128)(2,1)} %bitcast.116), channel_id=1, source_target_pairs={{0,2},{1,17},{16,18},{17,9},{8,10},{9,25},{24,26},{25,1},{2,4},{3,... | collective-permute-start | bytes 1179656 | tf_op jit(solution)/shard_map/ppermute | solution.py:43
  42.4 16.6 %collective-permute-start.25 = (bf16[128,1536]{1,0:T(8,128)(2,1)}, bf16[128,1536]{1,0:T(8,128)(2,1)}, u32[]{:S(2)}, u32[]{:S(2)}) collective-permute-start(bf16[128,1536]{1,0:T(8,128)(2,1)} %bitcast.117), channel_id=1, source_target_pairs={{0,4},{1,9},{16,20},{17,25},{8,12},{9,1},{24,28},{25,17},{2,6},{3,... | collective-permute-start | bytes 1179656 | tf_op jit(solution)/shard_map/ppermute | solution.py:43
  45.0 13.9 %collective-permute-start.26 = (bf16[128,1536]{1,0:T(8,128)(2,1)}, bf16[128,1536]{1,0:T(8,128)(2,1)}, u32[]{:S(2)}, u32[]{:S(2)}) collective-permute-start(bf16[128,1536]{1,0:T(8,128)(2,1)} %bitcast.118), channel_id=1, source_target_pairs={{0,6},{1,25},{16,22},{17,1},{8,14},{9,17},{24,30},{25,9},{2,0},{3,... | collective-permute-start | bytes 1179656 | tf_op jit(solution)/shard_map/ppermute | solution.py:43
  46.1 27.6 %collective-permute-start.13 = (bf16[192,1536]{1,0:T(8,128)(2,1)}, bf16[192,1536]{1,0:T(8,128)(2,1)}, u32[]{:S(2)}, u32[]{:S(2)}) collective-permute-start(bf16[192,1536]{1,0:T(8,128)(2,1)} %get-tuple-element.17), channel_id=1, source_target_pairs={{0,8},{1,7},{16,24},{17,23},{8,0},{9,15},{24,16},{25,31},{2,10},{3... | collective-permute-start | bytes 1769480 | tf_op jit(solution)/shard_map/ppermute | solution.py:43
  62.8 40.4 %collective-permute-start.27 = (bf16[192,1536]{1,0:T(8,128)(2,1)S(1)}, bf16[192,1536]{1,0:T(8,128)(2,1)S(1)}, u32[]{:S(2)}, u32[]{:S(2)}) collective-permute-start(bf16[192,1536]{1,0:T(8,128)(2,1)S(1)} %get-tuple-element.24), channel_id=1, source_target_pairs={{0,16},{1,5},{16,8},{17,21},{8,24},{9,13},{24,0},{25,29},{2,18},{3... | collective-permute-start | bytes 1769480 | tf_op jit(solution)/shard_map/ppermute | solution.py:43
  64.5 40.3 %collective-permute-start.28 = (bf16[192,1536]{1,0:T(8,128)(2,1)S(1)}, bf16[192,1536]{1,0:T(8,128)(2,1)S(1)}, u32[]{:S(2)}, u32[]{:S(2)}) collective-permute-start(bf16[192,1536]{1,0:T(8,128)(2,1)S(1)} %get-tuple-element.25), channel_id=1, source_target_pairs={{0,8},{1,7},{16,24},{17,23},{8,0},{9,15},{24,16},{25,31},{2,10},{3... | collective-permute-start | bytes 1769480 | tf_op jit(solution)/shard_map/ppermute | solution.py:43
  68.2 36.7 %collective-permute-start.29 = (bf16[192,1536]{1,0:T(8,128)(2,1)S(1)}, bf16[192,1536]{1,0:T(8,128)(2,1)S(1)}, u32[]{:S(2)}, u32[]{:S(2)}) collective-permute-start(bf16[192,1536]{1,0:T(8,128)(2,1)S(1)} %get-tuple-element.26), channel_id=1, source_target_pairs={{0,24},{1,3},{16,0},{17,19},{8,16},{9,11},{24,8},{25,27},{2,26},{3... | collective-permute-start | bytes 1769480 | tf_op jit(solution)/shard_map/ppermute | solution.py:43
  68.8 17.1 %collective-permute-start.9 = (bf16[192,1536]{1,0:T(8,128)(2,1)}, bf16[192,1536]{1,0:T(8,128)(2,1)S(1)}, u32[]{:S(2)}, u32[]{:S(2)}) collective-permute-start(bf16[192,1536]{1,0:T(8,128)(2,1)} %copy-done.12), channel_id=1, source_target_pairs={{0,16},{1,5},{16,8},{17,21},{8,24},{9,13},{24,0},{25,29},{2,18},{3... | collective-permute-start | bytes 1769480 | tf_op jit(solution)/shard_map/ppermute | solution.py:43
  73.7 18.3 %collective-permute-start.17 = (bf16[192,1536]{1,0:T(8,128)(2,1)S(1)}, bf16[192,1536]{1,0:T(8,128)(2,1)S(1)}, u32[]{:S(2)}, u32[]{:S(2)}) collective-permute-start(bf16[192,1536]{1,0:T(8,128)(2,1)S(1)} %copy-done.11), channel_id=1, source_target_pairs={{0,24},{1,3},{16,0},{17,19},{8,16},{9,11},{24,8},{25,27},{2,26},{3... | collective-permute-start | bytes 1769480 | tf_op jit(solution)/shard_map/ppermute | solution.py:43
  103.2 22.1 %collective-permute-start.30 = (bf16[192,1536]{1,0:T(8,128)(2,1)S(1)}, bf16[192,1536]{1,0:T(8,128)(2,1)S(1)}, u32[]{:S(2)}, u32[]{:S(2)}) collective-permute-start(bf16[192,1536]{1,0:T(8,128)(2,1)S(1)} %get-tuple-element.23.refs_0_), channel_id=1, source_target_pairs={{0,1},{1,0},{2,3},{3,2},{4,5},{5,4},{6,7},{7,6},{8,9},{9,8},{10,11... | collective-permute-start | bytes 1769480 | tf_op jit(solution)/shard_map/ppermute | solution.py:56
  103.3 23.2 %collective-permute-start.31 = (bf16[192,1536]{1,0:T(8,128)(2,1)S(1)}, bf16[192,1536]{1,0:T(8,128)(2,1)S(1)}, u32[]{:S(2)}, u32[]{:S(2)}) collective-permute-start(bf16[192,1536]{1,0:T(8,128)(2,1)S(1)} %collective-permute-done.27.refs_1_), channel_id=1, source_target_pairs={{0,1},{1,0},{2,3},{3,2},{4,5},{5,4},{6,7},{7,6},{8,9},{9,8},{10,11... | collective-permute-start | bytes 1769480 | tf_op jit(solution)/shard_map/ppermute | solution.py:56
  104.7 16.6 %collective-permute-start.16 = (bf16[192,1536]{1,0:T(8,128)(2,1)S(1)}, bf16[192,1536]{1,0:T(8,128)(2,1)S(1)}, u32[]{:S(2)}, u32[]{:S(2)}) collective-permute-start(bf16[192,1536]{1,0:T(8,128)(2,1)S(1)} %add_convert_fusion.1), channel_id=1, source_target_pairs={{0,8},{1,3},{16,24},{17,19},{8,0},{9,11},{24,16},{25,27},{2,10},{3... | collective-permute-start | bytes 1769480 | tf_op jit(solution)/shard_map/ppermute | solution.py:43
  105.0 16.4 %collective-permute-start.20 = (bf16[192,1536]{1,0:T(8,128)(2,1)S(1)}, bf16[192,1536]{1,0:T(8,128)(2,1)S(1)}, u32[]{:S(2)}, u32[]{:S(2)}) collective-permute-start(bf16[192,1536]{1,0:T(8,128)(2,1)S(1)} %add_convert_fusion), channel_id=1, source_target_pairs={{0,16},{1,7},{16,8},{17,23},{8,24},{9,15},{24,0},{25,31},{2,18},{3... | collective-permute-start | bytes 1769480 | tf_op jit(solution)/shard_map/ppermute | solution.py:43
  107.5 15.1 %collective-permute-start.12 = (bf16[192,1536]{1,0:T(8,128)(2,1)S(1)}, bf16[192,1536]{1,0:T(8,128)(2,1)S(1)}, u32[]{:S(2)}, u32[]{:S(2)}) collective-permute-start(bf16[192,1536]{1,0:T(8,128)(2,1)S(1)} %add_convert_fusion.2), channel_id=1, source_target_pairs={{0,24},{1,5},{16,0},{17,21},{8,16},{9,13},{24,8},{25,29},{2,26},{3... | collective-permute-start | bytes 1769480 | tf_op jit(solution)/shard_map/ppermute | solution.py:43
  121.4 18.8 %collective-permute-start.32 = (bf16[192,1536]{1,0:T(8,128)(2,1)S(1)}, bf16[192,1536]{1,0:T(8,128)(2,1)S(1)}, u32[]{:S(2)}, u32[]{:S(2)}) collective-permute-start(bf16[192,1536]{1,0:T(8,128)(2,1)S(1)} %collective-permute-done.28.refs_2_), channel_id=1, source_target_pairs={{0,1},{1,0},{2,3},{3,2},{4,5},{5,4},{6,7},{7,6},{8,9},{9,8},{10,11... | collective-permute-start | bytes 1769480 | tf_op jit(solution)/shard_map/ppermute | solution.py:56
  121.4 18.8 %collective-permute-start.33 = (bf16[192,1536]{1,0:T(8,128)(2,1)S(1)}, bf16[192,1536]{1,0:T(8,128)(2,1)S(1)}, u32[]{:S(2)}, u32[]{:S(2)}) collective-permute-start(bf16[192,1536]{1,0:T(8,128)(2,1)S(1)} %collective-permute-done.29.refs_3_), channel_id=1, source_target_pairs={{0,1},{1,0},{2,3},{3,2},{4,5},{5,4},{6,7},{7,6},{8,9},{9,8},{10,11... | collective-permute-start | bytes 1769480 | tf_op jit(solution)/shard_map/ppermute | solution.py:56
  124.9 24.4 %collective-permute-start.21 = (bf16[128,1536]{1,0:T(8,128)(2,1)S(1)}, bf16[128,1536]{1,0:T(8,128)(2,1)S(1)}, u32[]{:S(2)}, u32[]{:S(2)}) collective-permute-start(bf16[128,1536]{1,0:T(8,128)(2,1)S(1)} %get-tuple-element.20), channel_id=1, source_target_pairs={{0,6},{1,25},{16,22},{17,1},{8,14},{9,17},{24,30},{25,9},{2,0},{3,... | collective-permute-start | bytes 1179656 | tf_op jit(solution)/shard_map/ppermute | solution.py:43
  125.3 24.0 %collective-permute-start.22 = (bf16[128,1536]{1,0:T(8,128)(2,1)S(1)}, bf16[128,1536]{1,0:T(8,128)(2,1)S(1)}, u32[]{:S(2)}, u32[]{:S(2)}) collective-permute-start(bf16[128,1536]{1,0:T(8,128)(2,1)S(1)} %get-tuple-element.21), channel_id=1, source_target_pairs={{0,2},{1,17},{16,18},{17,9},{8,10},{9,25},{24,26},{25,1},{2,4},{3,... | collective-permute-start | bytes 1179656 | tf_op jit(solution)/shard_map/ppermute | solution.py:43
  126.5 22.9 %collective-permute-start.23 = (bf16[128,1536]{1,0:T(8,128)(2,1)S(1)}, bf16[128,1536]{1,0:T(8,128)(2,1)S(1)}, u32[]{:S(2)}, u32[]{:S(2)}) collective-permute-start(bf16[128,1536]{1,0:T(8,128)(2,1)S(1)} %get-tuple-element.22), channel_id=1, source_target_pairs={{0,4},{1,9},{16,20},{17,25},{8,12},{9,1},{24,28},{25,17},{2,6},{3,... | collective-permute-start | bytes 1179656 | tf_op jit(solution)/shard_map/ppermute | solution.py:43
  (26 other events, 155.9 us)
